TPU v7x, 512 devices: a whole 4x8x8 slice. The times are simulated.
512 devices in a mesh: rep: 32 (over z, x), tp: 16 (over y, core).
Axes of the slice: x: 4, y: 8, z: 8, core: 2. Of those that a mesh axis runs over, the one named last changes fastest.
Arguments:
- tokens: bfloat16 [16384, 8192], P('rep', 'tp'), may hold values from -6 to 6
- frozen_weight: bfloat16 [8192, 2048], P('tp'), may hold values from -0.0625 to 0.0625
- cotangent: bfloat16 [16384, 2048], P('rep', 'tp'), may hold values from -6 to 6
- adapter_input_maps: bfloat16 [32, 16, 8192], P('rep', None, 'tp'), may hold values from -0.0625 to 0.0625
- adapter_output_maps: bfloat16 [32, 16, 2048], P('rep', None, 'tp'), may hold values from -0.375 to 0.375
- tenant: int32 [128], P('rep'), may hold values from 0 to 31
- adapter_storage_slot: int32 [32], replicated, may hold values from 0 to 31, each once
Outputs:
- projected: float32 [16384, 2048], P('rep', 'tp')
- token_gradient: float32 [16384, 8192], P('rep', 'tp')
- adapter_input_gradient: float32 [32, 16, 8192], P('rep', None, 'tp')
- adapter_output_gradient: float32 [32, 16, 2048], P('rep', None, 'tp')
Inputs may be any that keep to these rules, and one draw needn't show every extreme that they name: `adapter_storage_slot`: each slot holds exactly one adapter.
All inputs are finite; a program needn't handle non-finite values.
Results may differ from a plain program's by a relative error of at most 0.00035.
Values may be sent and summed in bfloat16 or wider, within the bound.
A program may use at most 64 MiB of HBM per device.

v0:
```python
import jax
import jax.numpy as jnp
from jax import lax
from jax.sharding import PartitionSpec as P

HIGH_ACCURACY = lax.Precision.HIGHEST


def slot_lookup(tenants, adapter_storage_slot):
    labels = jnp.arange(adapter_storage_slot.shape[0], dtype=jnp.int32)
    return jnp.sum(
        jnp.where(tenants[:, None] == labels[None, :], adapter_storage_slot[None, :], 0), axis=1
    )


def shards(
    tokens,
    frozen_weight,
    cotangent,
    adapter_input_maps,
    adapter_output_maps,
    tenant,
    adapter_storage_slot,
):
    token_count = tokens.shape[0]
    blocks = tenant.shape[0]
    block_len = token_count // blocks
    tenant_token_count = adapter_input_maps.shape[0]
    inputs_all, outputs_all = (
        lax.all_gather(adapter_input_maps, "rep", axis=0, tiled=True),
        lax.all_gather(adapter_output_maps, "rep", axis=0, tiled=True),
    )
    adapter_list = inputs_all.shape[0]
    labels = jnp.arange(adapter_list, dtype=jnp.int32)
    block_storage_slot = slot_lookup(tenant, adapter_storage_slot)
    tenant_selector = (block_storage_slot[:, None] == labels[None, :]).astype(jnp.float32)
    picker = tenant_selector.astype(jnp.bfloat16)
    input_map_rows = jnp.einsum(
        "bs,srd->brd", picker, inputs_all, preferred_element_type=jnp.float32
    )
    output_map_rows = jnp.einsum(
        "bs,src->brc", picker, outputs_all, preferred_element_type=jnp.float32
    )
    token_rows = tokens.reshape(blocks, block_len, -1).astype(jnp.float32)
    grad_rows = cotangent.reshape(blocks, block_len, -1).astype(jnp.float32)
    part_in = jnp.einsum("bnd,brd->bnr", token_rows, input_map_rows, precision=HIGH_ACCURACY)
    part_back = jnp.einsum("bnc,brc->bnr", grad_rows, output_map_rows, precision=HIGH_ACCURACY)
    rank_in, rank_back = lax.psum((part_in, part_back), "tp")
    base_terms = jnp.dot(tokens, frozen_weight, preferred_element_type=jnp.float32)
    base = lax.psum_scatter(base_terms, "tp", scatter_dimension=1, tiled=True)
    low_rank = 2.0 * jnp.einsum("bnr,brc->bnc", rank_in, output_map_rows, precision=HIGH_ACCURACY)
    projected = base + low_rank.reshape(token_count, -1)
    through = lax.dot_general(
        lax.all_gather(cotangent, "tp", axis=1, tiled=True),
        frozen_weight,
        (((1,), (1,)), ((), ())),
        preferred_element_type=jnp.float32,
    )
    side = 2.0 * jnp.einsum("bnr,brd->bnd", rank_back, input_map_rows, precision=HIGH_ACCURACY)
    token_gradient = through + side.reshape(token_count, -1)
    input_map_gradient = 2.0 * jnp.einsum(
        "bnr,bnd->brd", rank_back, token_rows, precision=HIGH_ACCURACY
    )
    output_map_gradient = 2.0 * jnp.einsum(
        "bnr,bnc->brc", rank_in, grad_rows, precision=HIGH_ACCURACY
    )
    every_tenant = lax.all_gather(tenant, "rep", axis=0, tiled=True)
    every_slot = slot_lookup(every_tenant, adapter_storage_slot)
    owned = lax.axis_index("rep") * tenant_token_count + jnp.arange(
        tenant_token_count, dtype=jnp.int32
    )
    owner_select = (every_slot[:, None] == owned[None, :]).astype(jnp.float32)
    counts = block_len * jnp.sum(owner_select, axis=0)
    adapter_scale = 1.0 / jnp.maximum(counts, 1.0)
    table_in = jnp.einsum(
        "ol,oht->lht", tenant_selector, input_map_gradient, precision=HIGH_ACCURACY
    )
    table_out = jnp.einsum(
        "pa,pne->ane", tenant_selector, output_map_gradient, precision=HIGH_ACCURACY
    )
    input_gradient_sum, output_gradient_sum = (
        lax.psum_scatter(table_in, "rep", scatter_dimension=0, tiled=True),
        lax.psum_scatter(table_out, "rep", scatter_dimension=0, tiled=True),
    )
    adapter_input_gradient = input_gradient_sum * adapter_scale[:, None, None]
    adapter_output_gradient = output_gradient_sum * adapter_scale[:, None, None]
    return (projected, token_gradient, adapter_input_gradient, adapter_output_gradient)


def solution(mesh):
    placed = (
        P("rep", "tp"),
        P("tp", None),
        P("rep", "tp"),
        P("rep", None, "tp"),
        P("rep", None, "tp"),
        P("rep"),
        P(),
    )
    return jax.shard_map(
        shards,
        mesh=mesh,
        in_specs=placed,
        out_specs=(P("rep", "tp"), P("rep", "tp"), P("rep", None, "tp"), P("rep", None, "tp")),
        check_vma=False,
    )
```

profile of v0, /device:TPU:25, one launch (start us, length us, event | category | flops | bytes accessed | tf_op | source)
XLA Modules:
  0.0 783.0 jit_solution(3900021885987403363)
XLA Ops:
  7.2 0.0 copy-start
  7.2 0.0 copy-start.1
  7.2 0.0 copy-start.2
  7.2 0.0 all-reduce.4.cloned.1.call-start
  7.2 43.7 %all_gather.12 = bf16[32,16,512]{2,1,0:T(8,128)(2,1)S(1)} all-gather(bf16[1,16,512]{2,1,0:T(8,128)(2,1)} %param.10), channel_id=1, replica_groups=mesh['rep'=32,'tp'=16] {'rep'}, dimensions={0}, use_global_device_ids=true | all-gather | bytes 540672 | tf_op jit(solution)/shard_map/all_gather | solution.py:30
  50.9 32.8 %all_gather.13 = bf16[32,16,128]{2,1,0:T(8,128)(2,1)S(1)} all-gather(bf16[1,16,128]{2,1,0:T(8,128)(2,1)} %param.11), channel_id=1, replica_groups=mesh['rep'=32,'tp'=16] {'rep'}, dimensions={0}, use_global_device_ids=true | all-gather | bytes 135168 | tf_op jit(solution)/shard_map/all_gather | solution.py:31
  83.8 0.9 select_reduce_fusion.1
  84.6 0.4 fusion
  85.0 0.2 fusion.4
  85.2 2.2 convolution_bitcast_fusion.1
  87.4 0.0 copy-done.2
  87.4 0.9 convolution_bitcast_fusion
  88.3 0.0 all-reduce.4.cloned.1.call-update
  88.4 0.0 reduce-scatter.8.cloned.1.call-start
  88.4 124.0 %all-reduce.4.cloned.1.call-done = (f32[4,128,16]{1,2,0:T(8,128)}, f32[4,128,16]{1,2,0:T(8,128)}) async-done(((f32[4,128,16]{1,2,0:T(8,128)}, f32[4,128,16]{1,2,0:T(8,128)}), (f32[4,128,16]{1,2,0:T(8,128)}, f32[4,128,16]{1,2,0:T(8,128)})) %all-reduce.4.cloned.1.call-update) | async-done | bytes 65552 | tf_op jit(solution)/shard_map/psum | solution.py:48
  212.4 1.0 convolution_multiply_fusion.3
  213.4 0.4 fusion.8
  213.8 0.9 copy.36
  214.7 0.0 reduce-scatter.8.cloned.1.call-update
  214.7 0.0 reduce-scatter.6.cloned.1.call-start
  214.8 0.0 copy-done.1
  214.8 1.1 convolution_multiply_fusion.2
  215.8 0.7 fusion.2
  216.6 1.6 copy.34
  218.2 0.0 reduce-scatter.6.cloned.1.call-update
  218.2 0.0 all-gather.2.cloned.1.call-start
  218.2 0.5 all-gather.2.cloned.1.call-update
  218.8 0.0 reduce-scatter.4.cloned.1.call-start
  218.8 0.0 copy-done
  218.8 3.2 fusion.23
  222.0 0.0 reduce-scatter.4.cloned.1.call-update
  222.1 1.3 dynamic-slice
  224.0 0.0 copy-done.5
  224.0 0.2 dynamic-update-slice
  224.3 17.4 %all-reduce = s32[128]{0:T(128)S(1)} all-reduce(s32[128]{0:T(128)S(1)} %dynamic-update-slice), channel_id=1, replica_groups=mesh['rep'=32,'tp'=16] {'rep'}, use_global_device_ids=true, to_apply=%add | all-reduce | flops 128 | bytes 1024
  241.6 0.1 select_reduce_fusion
  241.7 0.6 fusion.22
  243.0 0.0 copy-done.3
  243.0 0.6 convolution_multiply_fusion.1
  243.6 2.0 convolution_multiply_fusion
  245.7 187.2 %reduce-scatter.8.cloned.1.call-done = f32[1,16,128]{2,1,0:T(8,128)} async-done(((f32[32,16,128]{2,1,0:T(8,128)}), f32[1,16,128]{2,1,0:T(8,128)}) %reduce-scatter.8.cloned.1.call-update) | async-done | bytes 8208 | tf_op jit(solution)/shard_map/reduce_scatter | solution.py:83
  432.9 1.3 broadcast_multiply_fusion.1
  434.2 224.1 %reduce-scatter.6.cloned.1.call-done = f32[1,16,512]{2,1,0:T(8,128)} async-done(((f32[32,16,512]{2,1,0:T(8,128)}), f32[1,16,512]{2,1,0:T(8,128)}) %reduce-scatter.6.cloned.1.call-update) | async-done | bytes 32784 | tf_op jit(solution)/shard_map/reduce_scatter | solution.py:82
  658.3 1.4 broadcast_multiply_fusion
  659.7 46.8 %all-gather.2.cloned.1.call-done = bf16[512,2048]{1,0:T(8,128)(2,1)} async-done(((bf16[512,128]{1,0:T(8,128)(2,1)}), bf16[512,2048]{1,0:T(8,128)(2,1)}) %all-gather.2.cloned.1.call-update) | async-done | bytes 2097168 | tf_op jit(solution)/shard_map/all_gather | solution.py:54
  706.5 4.1 convolution_add_fusion
  710.6 64.2 %reduce-scatter.4.cloned.1.call-done = f32[512,128]{1,0:T(8,128)} async-done(((f32[512,2048]{1,0:T(8,128)}), f32[512,128]{1,0:T(8,128)}) %reduce-scatter.4.cloned.1.call-update) | async-done | bytes 262160 | tf_op jit(solution)/shard_map/reduce_scatter | solution.py:50
  774.8 1.7 bitcast_add_fusion
  (7 shorter events, 0.0 us)
Async XLA Ops:
  7.2 211.7 %copy-start = (bf16[512,2048]{1,0:T(8,128)(2,1)S(1)}, bf16[512,2048]{1,0:T(8,128)(2,1)}, u32[]{:S(2)}) copy-start(bf16[512,2048]{1,0:T(8,128)(2,1)} %param.8) | copy-start | bytes 6291460
  7.2 207.6 %copy-start.1 = (bf16[512,512]{1,0:T(8,128)(2,1)S(1)}, bf16[512,512]{1,0:T(8,128)(2,1)}, u32[]{:S(2)}) copy-start(bf16[512,512]{1,0:T(8,128)(2,1)} %param.7) | copy-start | bytes 1572868
  7.2 80.2 %copy-start.2 = (bf16[512,128]{1,0:T(8,128)(2,1)S(1)}, bf16[512,128]{1,0:T(8,128)(2,1)}, u32[]{:S(2)}) copy-start(bf16[512,128]{1,0:T(8,128)(2,1)} %param.9) | copy-start | bytes 393220
  7.2 205.2 %all-reduce.4.cloned.1.call-start = ((), (), s32[]{:S(2)}) async-start(), calls=%async_computation.7 | async-start | bytes 131072 | tf_op jit(solution)/shard_map/psum | solution.py:48
  88.4 344.5 %reduce-scatter.8.cloned.1.call-start = ((), (), s32[]{:S(2)}) async-start(), calls=%async_computation.6 | async-start | bytes 270336 | tf_op jit(solution)/shard_map/reduce_scatter | solution.py:83
  214.7 443.6 %reduce-scatter.6.cloned.1.call-start = ((), (), s32[]{:S(2)}) async-start(), calls=%async_computation.5 | async-start | bytes 1081344 | tf_op jit(solution)/shard_map/reduce_scatter | solution.py:82
  218.2 488.3 %all-gather.2.cloned.1.call-start = ((), (), s32[]{:S(2)}) async-start(), calls=%async_computation.4 | async-start | bytes 2228224 | tf_op jit(solution)/shard_map/all_gather | solution.py:54
  218.8 556.1 %reduce-scatter.4.cloned.1.call-start = ((), (), s32[]{:S(2)}) async-start(), calls=%async_computation.3 | async-start | bytes 4456448 | tf_op jit(solution)/shard_map/reduce_scatter | solution.py:50
  222.0 2.0 copy-start.5
  222.0 19.6 %copy-start.6 = (s32[32]{0:T(128)S(1)}, s32[32]{0:T(128)}, u32[]{:S(2)}) copy-start(s32[32]{0:T(128)} %param.13) | copy-start | bytes 388
  222.0 21.0 %copy-start.3 = (f32[4,128,16]{1,2,0:T(8,128)S(1)}, f32[4,128,16]{1,2,0:T(8,128)}, u32[]{:S(2)}) copy-start(f32[4,128,16]{1,2,0:T(8,128)} %get-tuple-element.8) | copy-start | bytes 98308
  222.0 21.6 %copy-start.4 = (f32[4,128,16]{1,2,0:T(8,128)S(1)}, f32[4,128,16]{1,2,0:T(8,128)}, u32[]{:S(2)}) copy-start(f32[4,128,16]{1,2,0:T(8,128)} %get-tuple-element.9) | copy-start | bytes 98308
Sparse Core Ops, SparseCore 0:
  88.5 123.9 all-reduce.3
  217.4 215.4 reduce-scatter.7
  437.3 220.9 reduce-scatter.5
  660.2 46.2 all-gather.1
  709.2 65.6 reduce-scatter.3
where the time goes:
time: 784 us; the launch traced here: 783 us
  waiting for transfers between devices  647 us (83%)
  blocking collectives  93.9 us (12%)
  matrix products  16.8 us (2%)
  between operations  15.2 us (2%)
    reduce_scatter x1, waiting for transfers between devices, shards(): lax.psum_scatter(table_in, 'rep', scatter_dimension=0, tiled=True)  224 us
    reduce_scatter x1, waiting for transfers between devices, shards(): lax.psum_scatter(table_out, 'rep', scatter_dimension=0, tiled=True)  187 us
    psum x1, waiting for transfers between devices, shards(): rank_in, rank_back = lax.psum((part_in, part_back), 'tp')  124 us
    reduce_scatter x1, waiting for transfers between devices, shards(): base = lax.psum_scatter(base_terms, 'tp', scatter_dimension=1, tiled=True)  64.2 us
    all_gather x1, waiting for transfers between devices, shards(): lax.all_gather(cotangent, 'tp', axis=1, tiled=True)  46.8 us
    all_gather x1, blocking collectives, shards(): lax.all_gather(adapter_input_maps, 'rep', axis=0, tiled=True)  43.7 us
    all_gather x1, blocking collectives, shards(): lax.all_gather(adapter_output_maps, 'rep', axis=0, tiled=True)  32.8 us
    unnamed x1, blocking collectives  17.4 us
  transfers between devices with their start and end apart: 5, of which 5 were waited for; matrix products, arithmetic and copies ran while one was open for 2% of the time, Pallas kernels for 0%

commit v1 on v0

--- a/solution.py
+++ b/solution.py
@@ -28,7 +28,10 @@
     tenant_token_count = adapter_input_maps.shape[0]
     inputs_all, outputs_all = (
         lax.all_gather(adapter_input_maps, "rep", axis=0, tiled=True),
-        lax.all_gather(adapter_output_maps, "rep", axis=0, tiled=True),
+        jnp.concatenate(
+            lax.all_to_all(jnp.stack([adapter_output_maps] * lax.axis_size("rep")), "rep", 0, 0),
+            axis=0,
+        ),
     )
     adapter_list = inputs_all.shape[0]
     labels = jnp.arange(adapter_list, dtype=jnp.int32)

time: 784 us -> 753 us (0.960)
  blocking collectives: 93.9 us -> 56 us
  starting transfers between devices: 0.2 us -> 13.1 us
    all_gather x1 -> x0, blocking collectives: 32.8 us -> none  [shards(): lax.all_gather(adapter_output_maps, 'rep', axis=0, tiled=True)]
    all_to_all x0 -> x1, starting transfers between devices: none -> 12.9 us  [shards(): lax.all_to_all(jnp.stack([adapter_output_maps] * lax.axis_size('rep')), '...]
  transfers between devices with their start and end apart: 5 -> 6, of which waited for: 5 -> 5; matrix products, arithmetic and copies ran while one was open for 2% -> 3% of each run, Pallas kernels for 0% -> 0%
where the time goes in v1:
time: 753 us; the launch traced here: 752 us
  waiting for transfers between devices  640 us (85%)
  blocking collectives  56 us (7%)
  matrix products  16.8 us (2%)
  between operations  15.2 us (2%)
  starting transfers between devices  13.1 us (2%)
    reduce_scatter x1, waiting for transfers between devices, shards(): lax.psum_scatter(table_in, 'rep', scatter_dimension=0, tiled=True)  224 us
    reduce_scatter x1, waiting for transfers between devices, shards(): lax.psum_scatter(table_out, 'rep', scatter_dimension=0, tiled=True)  187 us
    psum x1, waiting for transfers between devices, shards(): rank_in, rank_back = lax.psum((part_in, part_back), 'tp')  117 us
    reduce_scatter x1, waiting for transfers between devices, shards(): base = lax.psum_scatter(base_terms, 'tp', scatter_dimension=1, tiled=True)  64.2 us
    all_gather x1, waiting for transfers between devices, shards(): lax.all_gather(cotangent, 'tp', axis=1, tiled=True)  46.8 us
    all_gather x1, blocking collectives, shards(): lax.all_gather(adapter_input_maps, 'rep', axis=0, tiled=True)  38.7 us
    unnamed x1, blocking collectives  17.4 us
  transfers between devices with their start and end apart: 6, of which 5 were waited for; matrix products, arithmetic and copies ran while one was open for 3% of the time, Pallas kernels for 0%

profile of v1, /device:TPU:25, one launch (start us, length us, event | category | flops | bytes accessed | tf_op | source)
XLA Modules:
  0.0 752.3 jit_solution(1125637772667302773)
XLA Ops:
  7.2 0.0 copy-start
  7.2 0.0 copy-start.1
  7.2 0.0 copy-start.2
  7.2 1.5 stack.2
  8.7 12.9 %all-to-all-start = ((bf16[32,1,16,128]{3,2,1,0:T(8,128)(2,1)}), bf16[32,1,16,128]{3,2,1,0:T(8,128)(2,1)S(1)}, u32[]{:S(2)}, u32[]{:S(2)}) async-start(bf16[32,1,16,128]{3,2,1,0:T(8,128)(2,1)} %stack.2), calls=%async_computation.1 | async-start | bytes 262144 | tf_op jit(solution)/shard_map/all_to_all | solution.py:32
  21.6 0.0 all-reduce.4.cloned.1.call-start
  21.7 38.7 %all_gather.9 = bf16[32,16,512]{2,1,0:T(8,128)(2,1)S(1)} all-gather(bf16[1,16,512]{2,1,0:T(8,128)(2,1)} %param.10), channel_id=1, replica_groups=mesh['rep'=32,'tp'=16] {'rep'}, dimensions={0}, use_global_device_ids=true | all-gather | bytes 540672 | tf_op jit(solution)/shard_map/all_gather | solution.py:30
  60.3 0.9 select_reduce_fusion.1
  61.2 0.4 fusion
  61.6 2.2 convolution_bitcast_fusion.1
  63.8 0.0 all-to-all-done
  63.8 0.2 fusion.2
  64.0 0.0 copy-done.2
  64.0 0.9 convolution_bitcast_fusion
  64.9 0.0 all-reduce.4.cloned.1.call-update
  64.9 0.0 reduce-scatter.8.cloned.1.call-start
  65.0 116.7 %all-reduce.4.cloned.1.call-done = (f32[4,128,16]{1,2,0:T(8,128)}, f32[4,128,16]{1,2,0:T(8,128)}) async-done(((f32[4,128,16]{1,2,0:T(8,128)}, f32[4,128,16]{1,2,0:T(8,128)}), (f32[4,128,16]{1,2,0:T(8,128)}, f32[4,128,16]{1,2,0:T(8,128)})) %all-reduce.4.cloned.1.call-update) | async-done | bytes 65552 | tf_op jit(solution)/shard_map/psum | solution.py:51
  181.7 1.0 convolution_multiply_fusion.3
  182.7 0.4 fusion.9
  183.1 0.9 copy.35
  184.0 0.0 reduce-scatter.8.cloned.1.call-update
  184.0 0.0 reduce-scatter.6.cloned.1.call-start
  184.1 0.0 copy-done.1
  184.1 1.1 convolution_multiply_fusion.2
  185.1 0.7 fusion.4
  185.9 1.6 copy.33
  187.5 0.0 reduce-scatter.6.cloned.1.call-update
  187.5 0.0 all-gather.2.cloned.1.call-start
  187.5 0.5 all-gather.2.cloned.1.call-update
  188.1 0.0 reduce-scatter.4.cloned.1.call-start
  188.1 0.0 copy-done
  188.1 3.2 fusion.24
  191.3 0.0 reduce-scatter.4.cloned.1.call-update
  191.4 1.3 dynamic-slice
  193.3 0.2 dynamic-update-slice
  193.6 17.4 %all-reduce = s32[128]{0:T(128)S(1)} all-reduce(s32[128]{0:T(128)S(1)} %dynamic-update-slice), channel_id=1, replica_groups=mesh['rep'=32,'tp'=16] {'rep'}, use_global_device_ids=true, to_apply=%add | all-reduce | flops 128 | bytes 1024
  210.9 0.1 select_reduce_fusion
  211.0 0.6 fusion.23
  212.3 0.6 convolution_multiply_fusion.1
  212.9 2.0 convolution_multiply_fusion
  214.9 187.2 %reduce-scatter.8.cloned.1.call-done = f32[1,16,128]{2,1,0:T(8,128)} async-done(((f32[32,16,128]{2,1,0:T(8,128)}), f32[1,16,128]{2,1,0:T(8,128)}) %reduce-scatter.8.cloned.1.call-update) | async-done | bytes 8208 | tf_op jit(solution)/shard_map/reduce_scatter | solution.py:86
  402.1 1.3 broadcast_multiply_fusion.1
  403.4 224.2 %reduce-scatter.6.cloned.1.call-done = f32[1,16,512]{2,1,0:T(8,128)} async-done(((f32[32,16,512]{2,1,0:T(8,128)}), f32[1,16,512]{2,1,0:T(8,128)}) %reduce-scatter.6.cloned.1.call-update) | async-done | bytes 32784 | tf_op jit(solution)/shard_map/reduce_scatter | solution.py:85
  627.6 1.4 broadcast_multiply_fusion
  629.0 46.8 %all-gather.2.cloned.1.call-done = bf16[512,2048]{1,0:T(8,128)(2,1)} async-done(((bf16[512,128]{1,0:T(8,128)(2,1)}), bf16[512,2048]{1,0:T(8,128)(2,1)}) %all-gather.2.cloned.1.call-update) | async-done | bytes 2097168 | tf_op jit(solution)/shard_map/all_gather | solution.py:57
  675.8 4.1 convolution_add_fusion
  679.9 64.2 %reduce-scatter.4.cloned.1.call-done = f32[512,128]{1,0:T(8,128)} async-done(((f32[512,2048]{1,0:T(8,128)}), f32[512,128]{1,0:T(8,128)}) %reduce-scatter.4.cloned.1.call-update) | async-done | bytes 262160 | tf_op jit(solution)/shard_map/reduce_scatter | solution.py:53
  744.1 1.7 bitcast_add_fusion
  (9 shorter events, 0.0 us)
Async XLA Ops:
  7.2 181.0 %copy-start = (bf16[512,2048]{1,0:T(8,128)(2,1)S(1)}, bf16[512,2048]{1,0:T(8,128)(2,1)}, u32[]{:S(2)}) copy-start(bf16[512,2048]{1,0:T(8,128)(2,1)} %param.8) | copy-start | bytes 6291460
  7.2 176.9 %copy-start.1 = (bf16[512,512]{1,0:T(8,128)(2,1)S(1)}, bf16[512,512]{1,0:T(8,128)(2,1)}, u32[]{:S(2)}) copy-start(bf16[512,512]{1,0:T(8,128)(2,1)} %param.7) | copy-start | bytes 1572868
  7.2 56.8 %copy-start.2 = (bf16[512,128]{1,0:T(8,128)(2,1)S(1)}, bf16[512,128]{1,0:T(8,128)(2,1)}, u32[]{:S(2)}) copy-start(bf16[512,128]{1,0:T(8,128)(2,1)} %param.9) | copy-start | bytes 393220
  8.7 55.0 %all-to-all-start = ((bf16[32,1,16,128]{3,2,1,0:T(8,128)(2,1)}), bf16[32,1,16,128]{3,2,1,0:T(8,128)(2,1)S(1)}, u32[]{:S(2)}, u32[]{:S(2)}) async-start(bf16[32,1,16,128]{3,2,1,0:T(8,128)(2,1)} %stack.2), calls=%async_computation.1 | async-start | bytes 262144 | tf_op jit(solution)/shard_map/all_to_all | solution.py:32
  21.6 160.1 %all-reduce.4.cloned.1.call-start = ((), (), s32[]{:S(2)}) async-start(), calls=%async_computation.8 | async-start | bytes 131072 | tf_op jit(solution)/shard_map/psum | solution.py:51
  64.9 337.2 %reduce-scatter.8.cloned.1.call-start = ((), (), s32[]{:S(2)}) async-start(), calls=%async_computation.7 | async-start | bytes 270336 | tf_op jit(solution)/shard_map/reduce_scatter | solution.py:86
  184.0 443.6 %reduce-scatter.6.cloned.1.call-start = ((), (), s32[]{:S(2)}) async-start(), calls=%async_computation.6 | async-start | bytes 1081344 | tf_op jit(solution)/shard_map/reduce_scatter | solution.py:85
  187.5 488.3 %all-gather.2.cloned.1.call-start = ((), (), s32[]{:S(2)}) async-start(), calls=%async_computation.5 | async-start | bytes 2228224 | tf_op jit(solution)/shard_map/all_gather | solution.py:57
  188.1 556.0 %reduce-scatter.4.cloned.1.call-start = ((), (), s32[]{:S(2)}) async-start(), calls=%async_computation.4 | async-start | bytes 4456448 | tf_op jit(solution)/shard_map/reduce_scatter | solution.py:53
  191.3 2.0 copy-start.5
  191.3 19.6 %copy-start.6 = (s32[32]{0:T(128)S(1)}, s32[32]{0:T(128)}, u32[]{:S(2)}) copy-start(s32[32]{0:T(128)} %param.13) | copy-start | bytes 388
  191.3 21.0 %copy-start.3 = (f32[4,128,16]{1,2,0:T(8,128)S(1)}, f32[4,128,16]{1,2,0:T(8,128)}, u32[]{:S(2)}) copy-start(f32[4,128,16]{1,2,0:T(8,128)} %get-tuple-element.8) | copy-start | bytes 98308
  191.3 21.6 %copy-start.4 = (f32[4,128,16]{1,2,0:T(8,128)S(1)}, f32[4,128,16]{1,2,0:T(8,128)}, u32[]{:S(2)}) copy-start(f32[4,128,16]{1,2,0:T(8,128)} %get-tuple-element.9) | copy-start | bytes 98308
Sparse Core Ops, SparseCore 0:
  65.1 116.6 all-reduce.3
  186.7 215.3 reduce-scatter.7
  406.5 221.0 reduce-scatter.5
  629.5 46.2 all-gather.1
  678.4 65.6 reduce-scatter.3
